TPU v7x, 32 devices: a whole 2x2x4 slice. The times are simulated.
32 devices in a mesh: groups: 2 (over y), seq: 4 (over z), inner: 2 (over x), head: 2 (over core).
Axes of the slice: x: 2, y: 2, z: 4, core: 2. Of those that a mesh axis runs over, the one named last changes fastest.
Arguments:
- queries: bfloat16 [2048, 32, 128], P(('groups', 'seq', 'inner'), 'head'), parts along dimension 0, as said below
- keys: bfloat16 [2048, 4, 128], P(('groups', 'seq', 'inner'), 'head'), parts along dimension 0
- values: bfloat16 [2048, 4, 128], P(('groups', 'seq', 'inner'), 'head'), parts along dimension 0, may hold values from -6 to 6
- log_decay: float32 [2048, 4], P(('groups', 'seq', 'inner'), 'head'), parts along dimension 0, as said below
- gain: float32 [32, 128], P('head'), may hold values from 0.1 to 1.9
- block_list: int32 [32, 16], P(('groups', 'seq', 'inner')), parts along dimension 0, may hold values from 0 to 15, as said below
Outputs:
- attended: bfloat16 [2048, 32, 128], P(('groups', 'seq', 'inner'), 'head'), parts along dimension 0
There are 2 independent parts, one for each index of `groups`. A program takes and returns all parts, laid end to end along the dimension named above; an argument that names none is the same for every part. Nothing has to cross between parts.
Inputs may be any that keep to these rules, and one draw needn't show every extreme that they name: Keys lie within -6 to 6; queries within -144 to 144. `log_decay`: each entry is below 0. `block_list`: entry 0 of row b is b. The sequence's pieces of 128 tokens fall into segments: piece p belongs to segment p modulo 2. Every entry of row b is a block at or before b in a piece of b's segment.
All inputs are finite; a program needn't handle non-finite values.
Results may differ from a plain program's by a relative error of at most 0.0017.
Values may be sent and summed in bfloat16 or wider, within the bound.
A program may use at most 64 MiB of HBM per device.

v0:
```python
import jax
import jax.numpy as jnp
from jax import lax
from jax.sharding import PartitionSpec as P

BLK = 64
SEL = 16


HIGH = lax.Precision.HIGHEST


def prefix(shard, axis, combine, identity):
    devices, here = (lax.axis_size(axis), lax.axis_index(axis))
    everything = jax.tree.map(lambda part: lax.all_gather(part, axis), shard)
    start = jax.tree.map(
        lambda part, zero: jnp.broadcast_to(jnp.asarray(zero, part.dtype), part.shape),
        shard,
        identity,
    )

    def turn(k, before):
        reached = k < here
        new = combine(before, jax.tree.map(lambda part: part[k], everything))
        return jax.tree.map(lambda a, b: jnp.where(reached, a, b), new, before)

    return lax.fori_loop(0, devices, turn, start)


def combine(earlier, later):
    return (earlier[0] * later[0], later[0][:, None, None] * earlier[1] + later[1])


def shards(queries, keys, values, log_decay, gain, block_list):
    tokens, heads_loc, width = queries.shape
    kv_loc = keys.shape[1]
    rep = heads_loc // kv_loc
    qf = queries.astype(jnp.float32).reshape(tokens, kv_loc, rep, width)
    kf = keys.astype(jnp.float32)
    vf = values.astype(jnp.float32)
    cum = jnp.cumsum(log_decay, axis=0)
    total = cum[-1]
    causal = jnp.arange(tokens)[:, None] >= jnp.arange(tokens)[None, :]
    scores = jnp.einsum("tkrd,skd->krts", qf, kf, precision=HIGH)
    diff = cum.T[:, :, None] - cum.T[:, None, :]
    weight = jnp.where(causal[None], jnp.exp(jnp.minimum(diff, 0.0)), 0.0)
    intra = jnp.einsum("krts,skd->tkrd", scores * weight[:, None], vf, precision=HIGH)
    tail = jnp.exp(total[None, :] - cum)
    own_state = jnp.einsum("skd,ske->kde", kf * tail[:, :, None], vf, precision=HIGH)
    own_decay = jnp.exp(total)
    identity = (jnp.ones_like(own_decay), jnp.zeros_like(own_state))
    prior = prefix((own_decay, own_state), ("seq", "inner"), combine, identity)
    prior_state = prior[1]
    inter = jnp.exp(cum)[:, :, None, None] * jnp.einsum(
        "tkrd,kde->tkre", qf, prior_state, precision=HIGH
    )
    linear = (intra + inter).reshape(tokens, heads_loc, width)
    normed = (
        linear * lax.rsqrt(jnp.mean(linear * linear, axis=-1, keepdims=True) + 1e-06) * gain[None]
    )
    per_piece = tokens // BLK
    n_inner = lax.axis_size("inner")
    start_pos = (lax.axis_index("seq") * n_inner + lax.axis_index("inner")) * tokens
    seg_block = block_list // (n_inner * per_piece) * per_piece + block_list % per_piece
    seg_keys, seg_values = (
        lax.all_gather(keys, "seq", axis=0, tiled=True),
        lax.all_gather(values, "seq", axis=0, tiled=True),
    )
    key_blocks = seg_keys.reshape(-1, BLK, kv_loc, width)
    value_blocks = seg_values.reshape(-1, BLK, kv_loc, width)
    picked_keys = key_blocks[seg_block]
    picked_values = value_blocks[seg_block]
    lower = jnp.arange(SEL)[None, :] < jnp.arange(SEL)[:, None]
    repeat = jnp.any((block_list[:, :, None] == block_list[:, None, :]) & lower[None], axis=2)
    keep_all = jnp.logical_not(repeat)
    query_pos = start_pos + jnp.arange(tokens).reshape(per_piece, BLK)
    key_pos = block_list[:, :, None] * BLK + jnp.arange(BLK)[None, None, :]
    q_blocks = queries.reshape(per_piece, BLK, kv_loc, rep, width)

    def one_block(args):
        qblk, pk, pv, qpos, kpos, keep = args
        valid = keep[None, :, None] & (kpos[None] <= qpos[:, None, None])
        score = jnp.einsum(
            "qkrd,jukd->krqju", qblk, pk, preferred_element_type=jnp.float32
        ) * width ** (-0.5)
        score = jnp.where(valid[None, None], score, -1e30)
        top = jnp.max(score, axis=(3, 4), keepdims=True)
        expo = jnp.where(valid[None, None], jnp.exp(score - top), 0.0)
        denom = jnp.sum(expo, axis=(3, 4))
        weights = expo.astype(jnp.bfloat16)
        out = jnp.einsum("krqju,jukd->qkrd", weights, pv, preferred_element_type=jnp.float32)
        return out / jnp.transpose(denom, (2, 0, 1))[:, :, :, None]

    outs = lax.map(one_block, (q_blocks, picked_keys, picked_values, query_pos, key_pos, keep_all))
    sparse = outs.reshape(tokens, heads_loc, width)
    return (normed + sparse).astype(jnp.bfloat16)


def solution(mesh):
    return jax.shard_map(
        shards,
        mesh=mesh,
        in_specs=(
            P(("groups", "seq", "inner"), "head", None),
            P(("groups", "seq", "inner"), "head", None),
            P(("groups", "seq", "inner"), "head", None),
            P(("groups", "seq", "inner"), "head"),
            P("head", None),
            P(("groups", "seq", "inner"), None),
        ),
        out_specs=P(("groups", "seq", "inner"), "head", None),
        check_vma=False,
    )
```

profile of v0, /device:TPU:0, one launch (start us, length us, event | category | flops | bytes accessed | tf_op | source)
XLA Modules:
  0.0 109.6 jit_solution(16745564901405145584)
XLA Ops:
  6.5 0.8 copy.113
  8.1 1.0 convert_multiply_fusion
  9.2 1.8 %fusion.30 = f32[2,128,128]{2,1,0:T(8,128)} fusion(f32[128,2,128]{2,1,0:T(2,128)S(1)} %convert_multiply_fusion, bf16[128,2,128]{2,1,0:T(2,128)(2,1)} %param.12), kind=kOutput, calls=%fused_computation.44 | convolution fusion | flops 50331648 | bytes 327680 | tf_op jit(solution)/shard_map/skd,ske->kde/dot_general | solution.py:49
  11.0 0.9 copy.121
  11.9 0.9 copy.129
  12.7 16.1 %all_gather.19 = bf16[512,2,128]{2,0,1:T(8,128)(2,1)S(1)} all-gather(bf16[128,2,128]{2,0,1:T(8,128)(2,1)S(1)} %copy.121), channel_id=1, replica_groups=mesh['groups'=2,'seq'=4,'inner'=2,'head'=2] {'seq'}, dimensions={0}, use_global_device_ids=true | all-gather | bytes 327680 | tf_op jit(solution)/shard_map/all_gather | solution.py:67
  29.6 0.9 and_reduce_fusion
  31.8 15.7 %all_gather.20 = bf16[512,2,128]{2,0,1:T(8,128)(2,1)S(1)} all-gather(bf16[128,2,128]{2,0,1:T(8,128)(2,1)S(1)} %copy.129), channel_id=1, replica_groups=mesh['groups'=2,'seq'=4,'inner'=2,'head'=2] {'seq'}, dimensions={0}, use_global_device_ids=true | all-gather | bytes 327680 | tf_op jit(solution)/shard_map/all_gather | solution.py:66
  47.5 0.7 gather_fusion
  48.2 0.9 gather_fusion.1
  49.2 18.8 %while.24 = (s32[]{:T(128)}, f32[2,64,2,8,128]{4,3,2,1,0:T(8,128)S(1)}, bf16[2,16,64,2,128]{4,2,3,1,0:T(8,128)(2,1)S(1)}, pred[2,16]{1,0:T(4,128)(4,1)}, s32[2,1...) while((s32[]{:T(128)}, ...), condition=%wide.region_8.9_spmd, body=%wide.region_5.8_spmd.sunk | while | flops 550762496 | bytes 18383788 | solution.py:94
  50.8 1.0 constant_dynamic-slice_fusion.7
  51.8 1.8 %fusion.49 = (f32[2,8,64]{2,1,0:T(8,128)S(1)}, f32[2,16,64,64,8]{3,2,4,1,0:T(8,128)S(1)}) fusion(pred[64,16,64]{0,2,1:T(8,128)(4,1)S(1)} %compare_and_fusion.2, bf16[1,64,2,8,128]{4,3,2,1,0:T(8,128)(2,1)S(1)} %constant_dynamic-slice_fusion.7, bf16[1,16,64,2,128]{4,2,3,1,0:T(8,128)(2,1)S(1)} %get-tuple-element.348), kind=kOutput, calls=%fused_computation.4.clone.1 | convolution fusion | flops 271580160 | bytes 5050368 | tf_op jit(solution)/shard_map/while/body/eval_jaxpr/qkrd,jukd->krqju/dot_general | solution.py:83
  53.6 2.3 %fusion.50 = f32[2,8,64]{2,1,0:T(8,128)S(1)} fusion(f32[2,16,64,64,8]{3,2,4,1,0:T(8,128)S(1)} %get-tuple-element.349, f32[2,8,64]{2,1,0:T(8,128)S(1)} %get-tuple-element.350, pred[64,16,64]{0,2,1:T(8,128)(4,1)S(1)} %compare_and_fusion.2), kind=kLoop, calls=%fused_computation.5.clone.1 | loop fusion | flops 5241856 | bytes 4268032 | tf_op jit(solution)/shard_map/while/body/eval_jaxpr/reduce_sum | solution.py:89
  55.9 2.3 %fusion.51 = f32[1,64,2,8,128]{4,1,3,2,0:T(8,128)S(1)} fusion(f32[2,16,64,64,8]{3,2,4,1,0:T(8,128)S(1)} %get-tuple-element.349, f32[2,8,64]{2,1,0:T(8,128)S(1)} %get-tuple-element.350, pred[64,16,64]{0,2,1:T(8,128)(4,1)S(1)} %compare_and_fusion.2, bf16[1,16,64,2,128]{4,2,3,1,0:T(8,128)(2,1)S(1)} %get-tuple-element.351, f32[64,2,8]{0,2,1:T(8,128)S(1)} %bitcast.148), kind=kOutput, calls=%fused_computation.11.clone.1 | convolution fusion | flops 273809408 | bytes 5316608 | tf_op jit(solution)/shard_map/while/body/eval_jaxpr/krqju,jukd->qkrd/dot_general | solution.py:91
  60.2 1.0 constant_dynamic-slice_fusion.7
  61.2 1.8 %fusion.49 = (f32[2,8,64]{2,1,0:T(8,128)S(1)}, f32[2,16,64,64,8]{3,2,4,1,0:T(8,128)S(1)}) fusion(pred[64,16,64]{0,2,1:T(8,128)(4,1)S(1)} %compare_and_fusion.2, bf16[1,64,2,8,128]{4,3,2,1,0:T(8,128)(2,1)S(1)} %constant_dynamic-slice_fusion.7, bf16[1,16,64,2,128]{4,2,3,1,0:T(8,128)(2,1)S(1)} %get-tuple-element.348), kind=kOutput, calls=%fused_computation.4.clone.1 | convolution fusion | flops 271580160 | bytes 5050368 | tf_op jit(solution)/shard_map/while/body/eval_jaxpr/qkrd,jukd->krqju/dot_general | solution.py:83
  63.0 2.3 %fusion.50 = f32[2,8,64]{2,1,0:T(8,128)S(1)} fusion(f32[2,16,64,64,8]{3,2,4,1,0:T(8,128)S(1)} %get-tuple-element.349, f32[2,8,64]{2,1,0:T(8,128)S(1)} %get-tuple-element.350, pred[64,16,64]{0,2,1:T(8,128)(4,1)S(1)} %compare_and_fusion.2), kind=kLoop, calls=%fused_computation.5.clone.1 | loop fusion | flops 5241856 | bytes 4268032 | tf_op jit(solution)/shard_map/while/body/eval_jaxpr/reduce_sum | solution.py:89
  65.3 2.3 %fusion.51 = f32[1,64,2,8,128]{4,1,3,2,0:T(8,128)S(1)} fusion(f32[2,16,64,64,8]{3,2,4,1,0:T(8,128)S(1)} %get-tuple-element.349, f32[2,8,64]{2,1,0:T(8,128)S(1)} %get-tuple-element.350, pred[64,16,64]{0,2,1:T(8,128)(4,1)S(1)} %compare_and_fusion.2, bf16[1,16,64,2,128]{4,2,3,1,0:T(8,128)(2,1)S(1)} %get-tuple-element.351, f32[64,2,8]{0,2,1:T(8,128)S(1)} %bitcast.148), kind=kOutput, calls=%fused_computation.11.clone.1 | convolution fusion | flops 273809408 | bytes 5316608 | tf_op jit(solution)/shard_map/while/body/eval_jaxpr/krqju,jukd->qkrd/dot_general | solution.py:91
  68.0 20.6 %all-gather.1 = f32[8,1,2]{2,1,0:T(1,128)S(1)} all-gather(f32[1,1,2]{2,1,0:T(1,128)S(1)} %copy-done.4), channel_id=1, replica_groups=mesh['groups'=2,'seq'=4,'inner'=2,'head'=2] {'seq','inner'}, dimensions={0}, use_global_device_ids=true | all-gather | bytes 72 | tf_op jit(solution)/shard_map/all_gather | solution.py:15
  88.9 1.4 %fusion.26 = f32[2,8,128,128]{2,3,1,0:T(8,128)S(1)} fusion(f32[2,128,128]{1,2,0:T(8,128)S(1)} %exponential_select_fusion.1, bf16[128,2,8,128]{3,2,1,0:T(8,128)(2,1)} %bitcast.138, bf16[128,2,128,1]{2,1,0,3:T(2,128)(2,1)S(1)} %bitcast.144), kind=kOutput, calls=%fused_computation.38 | convolution fusion | flops 67371008 | bytes 1769472 | tf_op jit(solution)/shard_map/tkrd,skd->krts/dot_general | solution.py:44
  91.0 8.3 %while.25 = (s32[]{:T(128)}, f32[2,128,128]{2,1,0:T(8,128)S(1)}, s32[]{:T(128)}, f32[8,2]{1,0:T(8,128)S(1)}, f32[8,2,128,128]{3,2,1,0:T(8,128)}, /*index=5*/s32[]{:T(128)}, s32[]{:T(128)}) while((s32[]{:T(128)}, f32[2,128,128]{2,1,0:T(8,128)S(1)}, s32[]{:T(128)}, f32[8,2]{1,0:T(8,128)S(1)}, f32[8,2,128,128]{3,2,1,0:T(8,128)}, ...), condition=%wide.region_2.3_spmd.clone, body=%wide.region_1.2_spmd.clone.sunk | while | flops 131076 | bytes 393353 | solution.py:27
  91.0 1.0 fusion.52
  92.0 1.0 fusion.52
  93.1 1.0 fusion.52
  94.1 1.0 fusion.52
  95.1 1.0 fusion.52
  96.2 1.0 fusion.52
  97.2 1.0 fusion.52
  98.2 1.0 fusion.52
  99.2 1.8 %multiply_reduce_fusion = (f32[128,2,8]{0,2,1:T(8,128)S(1)}, f32[128,2,8,128]{0,3,2,1:T(8,128)S(1)}) fusion(f32[128,2,8,128]{0,3,2,1:T(8,128)S(1)} %convolution_bitcast_fusion.2, bf16[128,2,8,128]{3,2,1,0:T(8,128)(2,1)} %bitcast.139, f32[2,128,128]{2,1,0:T(8,128)S(1)} %get-tuple-element.141, f32[128,2]{0,1:T(2,128)S(1)} %copy.118), kind=kOutput, calls=%fused_computation.40 | convolution fusion | flops 403699712 | bytes 2761728 | tf_op jit(solution)/shard_map/tkrd,kde->tkre/dot_general | solution.py:54
  101.6 1.1 %add_convert_fusion = bf16[128,16,128]{2,1,0:T(8,128)(2,1)} fusion(f32[128,16,128]{2,1,0:T(8,128)S(1)} %bitcast.143, f32[128,16,128]{2,1,0:T(8,128)S(1)} %copy.126, f32[16,128]{1,0:T(8,128)S(1)} %copy-done.3, f32[128,16]{1,0:T(8,128)S(1)} %copy.125), kind=kLoop, calls=%fused_computation.39 | loop fusion | flops 1048576 | bytes 2637824 | tf_op jit(solution)/shard_map/convert_element_type | solution.py:96
  (55 shorter events, 8.6 us)
Async XLA Ops:
  6.5 84.4 %all-gather.4.cloned.1.call-start = ((), (), s32[]{:S(2)}) async-start(), calls=%async_computation | async-start | bytes 1179648 | tf_op jit(solution)/shard_map/all_gather | solution.py:15
  29.6 17.9 %copy-start.2 = (s32[1024]{0:T(1024)}, s32[1024]{0:T(1024)S(1)}, u32[]{:S(2)}) copy-start(s32[1024]{0:T(1024)S(1)} %pad_clamp_fusion) | copy-start | bytes 12292
  49.1 18.8 %copy-start.4 = (f32[1,1,2]{2,1,0:T(1,128)S(1)}, f32[1,1,2]{2,1,0:T(1,128)}, u32[]{:S(2)}) copy-start(f32[1,1,2]{2,1,0:T(1,128)} %get-tuple-element.264) | copy-start | bytes 28
  49.1 39.7 %copy-start = (bf16[128,2,128]{2,1,0:T(2,128)(2,1)S(1)}, bf16[128,2,128]{2,1,0:T(2,128)(2,1)}, u32[]{:S(2)}) copy-start(bf16[128,2,128]{2,1,0:T(2,128)(2,1)} %param.11) | copy-start | bytes 196612
  49.2 41.1 %copy-start.1 = (bf16[128,2,128]{2,1,0:T(2,128)(2,1)S(1)}, bf16[128,2,128]{2,1,0:T(2,128)(2,1)}, u32[]{:S(2)}) copy-start(bf16[128,2,128]{2,1,0:T(2,128)(2,1)} %param.12) | copy-start | bytes 196612
  67.9 33.7 %copy-start.3 = (f32[16,128]{1,0:T(8,128)S(1)}, f32[16,128]{1,0:T(8,128)}, u32[]{:S(2)}) copy-start(f32[16,128]{1,0:T(8,128)} %param.14) | copy-start | bytes 24580
Sparse Core Ops, SparseCore 0:
  11.1 43.3 all-gather.3
where the time goes:
time: 110 us
  blocking collectives  52.4 us (48%)
  other arithmetic  18.3 us (17%)
  matrix products  13.7 us (12%)
  between operations  13.6 us (12%)
  local copies, waits for them, and re-layouts  11.2 us (10%)
    all_gather x1, blocking collectives, prefix(): everything = jax.tree.map(lambda part: lax.all_gather(part, axis), shard)  20.6 us
    all_gather x1, blocking collectives, shards(): lax.all_gather(values, 'seq', axis=0, tiled=True)  16.1 us
    all_gather x1, blocking collectives, shards(): lax.all_gather(keys, 'seq', axis=0, tiled=True)  15.7 us
    select_n x8, other arithmetic, turn(): return jax.tree.map(lambda a, b: jnp.where(reached, a, b), new, before)  7.94 us
    dot_general x2, matrix products, one_block(): jnp.einsum('krqju,jukd->qkrd', weights, pv, preferred_element_type=jnp.fl...  4.6 us
    reduce_sum x2, other arithmetic, one_block(): denom = jnp.sum(expo, axis=(3, 4))  4.54 us
    dot_general x2, matrix products, one_block(): jnp.einsum('qkrd,jukd->krqju', qblk, pk, preferred_element_type=jnp.float32)  3.54 us
    unnamed x13, local copies, waits for them, and re-layouts  2.52 us
  transfers between devices with their start and end apart: 1, of which 0 were waited for; matrix products, arithmetic and copies ran while one was open for 25% of the time, Pallas kernels for 0%

commit v1 on v0

v1 whole, which is shorter than its diff:
```python
import functools

import jax
import jax.numpy as jnp
from jax import lax
from jax.experimental import pallas as pl
from jax.experimental.pallas import tpu as pltpu
from jax.sharding import PartitionSpec as P

BLK = 64
HIGH = lax.Precision.HIGHEST
MESH = pl.DeviceIdType.MESH
LD_ROWS = 8
F32 = jnp.float32
BF16 = jnp.bfloat16
LOG2E = 1.4426950408889634


def iota(shape, dim):
    return lax.broadcasted_iota(jnp.int32, shape, dim)


def dot(a, b, dims=((1,), (0,)), precision=None):
    return lax.dot_general(
        a, b, (dims, ((), ())), precision=precision, preferred_element_type=F32
    )


def halves(x):
    hi = x.astype(BF16)
    return hi, (x - hi.astype(F32)).astype(BF16)


def kernel(
    n_seq, n_inner, kv,
    q_hbm, k_hbm, v_hbm, ld_ref, gain_ref, list_ref,
    out_ref,
    qbuf, kbuf, vbuf, ldbuf, qs, kd, vd, bias, lin, sp, msg, got,
    local_sem, k_send, k_recv, v_send, v_recv, ld_send, ld_recv, m_send, m_recv,
):
    z = lax.axis_index("seq")
    x = lax.axis_index("inner")
    pieces = n_seq * n_inner
    tokens, heads, width = qbuf.shape
    rep = heads // kv
    rows = tokens * rep
    per_piece = tokens // BLK
    keys_all = n_seq * tokens

    q_copy = pltpu.make_async_copy(q_hbm, qbuf, local_sem.at[0])
    k_copy = pltpu.make_async_copy(k_hbm, kbuf.at[z], local_sem.at[1])
    v_copy = pltpu.make_async_copy(v_hbm, vbuf.at[z], local_sem.at[2])
    l_copy = pltpu.make_async_copy(ld_ref, ldbuf.at[z * n_inner], local_sem.at[3])
    for copy in (k_copy, v_copy, l_copy, q_copy):
        copy.start()

    me = z * n_inner + x
    barrier = pltpu.get_barrier_semaphore()

    @pl.loop(1, pieces)
    def _(o):
        p = lax.rem(me + o, pieces)
        pl.semaphore_signal(
            barrier, inc=1, device_id={"seq": p // n_inner, "inner": lax.rem(p, n_inner)},
            device_id_type=MESH)

    pl.semaphore_wait(barrier, pieces - 1)

    def kv_copies(o):
        to = {"seq": lax.rem(z + o, n_seq)}
        return (
            pltpu.make_async_remote_copy(
                src_ref=k_hbm, dst_ref=kbuf.at[z], send_sem=k_send.at[o],
                recv_sem=k_recv.at[o], device_id=to, device_id_type=MESH),
            pltpu.make_async_remote_copy(
                src_ref=v_hbm, dst_ref=vbuf.at[z], send_sem=v_send.at[o],
                recv_sem=v_recv.at[o], device_id=to, device_id_type=MESH),
        )

    def ld_copy(o):
        oz, ox = o // n_inner, lax.rem(o, n_inner)
        slot = z * n_inner + lax.rem(n_inner - ox, n_inner)
        return pltpu.make_async_remote_copy(
            src_ref=ld_ref, dst_ref=ldbuf.at[slot], send_sem=ld_send.at[o],
            recv_sem=ld_recv.at[o],
            device_id={"seq": lax.rem(z + oz, n_seq), "inner": lax.rem(x + ox, n_inner)},
            device_id_type=MESH)

    def ld_arrival(o):
        oz, ox = o // n_inner, lax.rem(o, n_inner)
        slot = lax.rem(z + n_seq - oz, n_seq) * n_inner + lax.rem(n_inner - ox, n_inner)
        return pltpu.make_async_remote_copy(
            src_ref=ld_ref, dst_ref=ldbuf.at[slot], send_sem=ld_send.at[o],
            recv_sem=ld_recv.at[o], device_id={"seq": z}, device_id_type=MESH)

    def kv_arrivals(o):
        slot = lax.rem(z + n_seq - o, n_seq)
        return (
            pltpu.make_async_remote_copy(
                src_ref=k_hbm, dst_ref=kbuf.at[slot], send_sem=k_send.at[o],
                recv_sem=k_recv.at[o], device_id={"seq": z}, device_id_type=MESH),
            pltpu.make_async_remote_copy(
                src_ref=v_hbm, dst_ref=vbuf.at[slot], send_sem=v_send.at[o],
                recv_sem=v_recv.at[o], device_id={"seq": z}, device_id_type=MESH),
        )

    @pl.loop(1, pieces)
    def _(o):
        ld_copy(o).start()

    for o in range(1, n_seq):
        for copy in kv_copies(o):
            copy.start()

    lanes = iota((kv * tokens, kv * tokens), 1)
    subs = iota((kv * tokens, kv * tokens), 0)
    by_head = jnp.where(
        lanes == lax.rem(subs, tokens) * kv + subs // tokens, 1.0, 0.0
    ).astype(BF16)

    ld = ld_ref[...]
    upto = jnp.where(iota((tokens, tokens), 0) <= iota((tokens, tokens), 1), 1.0, 0.0)
    cum_lane = dot(ld, upto, precision=HIGH)
    row_tok = iota((rows, tokens), 0) // rep
    lane_tok = iota((rows, tokens), 1)
    seen = row_tok >= lane_tok
    cum_row = dot(jnp.where(seen, 1.0, 0.0), ld, ((1,), (1,)), HIGH)

    k_copy.wait()
    v_copy.wait()
    k_own = dot(by_head, kbuf[z]).astype(BF16)
    v_own = dot(by_head, vbuf[z]).astype(BF16)
    q_copy.wait()
    qf = qbuf[...].astype(F32)
    for g in range(kv):
        q_g = qf[:, g * rep:(g + 1) * rep, :].reshape(rows, width).astype(BF16)
        qs[g] = q_g
        k_g = k_own[g * tokens:(g + 1) * tokens]
        v_g = v_own[g * tokens:(g + 1) * tokens]
        diff = cum_row[:, g:g + 1] - cum_lane[g:g + 1, :]
        weight = jnp.where(seen, jnp.exp(jnp.minimum(diff, 0.0)), 0.0)
        hi, lo = halves(dot(q_g, k_g, ((1,), (1,))) * weight)
        lin[g] = dot(
            jnp.concatenate([hi, lo], axis=1), jnp.concatenate([v_g, v_g], axis=0))

    key_lane = iota((1, keys_all), 1)
    key_block = (
        (key_lane // tokens * n_inner + x) * per_piece + lax.rem(key_lane, tokens) // BLK
    )
    key_pos = key_block * BLK + lax.rem(key_lane, BLK)
    listed = list_ref[...]
    for b in range(per_piece):
        member = key_block == listed[b:b + 1, 0:1]
        for i in range(1, listed.shape[1]):
            member = jnp.logical_or(member, key_block == listed[b:b + 1, i:i + 1])
        limit = jnp.where(member, key_pos, jnp.int32(2**30))
        query = me * tokens + b * BLK + iota((BLK * rep, 1), 0) // rep
        bias[b * BLK * rep:(b + 1) * BLK * rep, :] = jnp.where(limit <= query, 0.0, -1e30)

    l_copy.wait()

    @pl.loop(1, pieces)
    def _(o):
        ld_arrival(o).wait_recv()

    n_ld = pieces * LD_ROWS
    ld_all = ldbuf[...].reshape(n_ld, tokens)
    after = jnp.where(iota((tokens, tokens), 0) < iota((tokens, tokens), 1), 1.0, 0.0)
    tail = dot(after, ld_all, ((1,), (1,)), HIGH)
    total = dot(jnp.ones((8, tokens), F32), ld_all, ((1,), (1,)), HIGH)[0:1]

    def piece_of(r):
        i = r // LD_ROWS
        return i // n_inner * n_inner + lax.rem(x + lax.rem(i, n_inner), n_inner)

    r0, r1 = iota((n_ld, n_ld), 0), iota((n_ld, n_ld), 1)
    between = (
        (lax.rem(r0, LD_ROWS) == lax.rem(r1, LD_ROWS))
        & (piece_of(r0) > piece_of(r1)) & (piece_of(r0) < z * n_inner)
    )
    rest = dot(
        jnp.broadcast_to(total, (8, n_ld)), jnp.where(between, 1.0, 0.0), precision=HIGH
    )[0:1]
    r = iota((1, n_ld), 1)
    far = jnp.where(piece_of(r) < z * n_inner, jnp.exp(tail + rest), 0.0)

    def span(g, first, last):
        inside = (lax.rem(r, LD_ROWS) == g) & (piece_of(r) >= first) & (piece_of(r) < last)
        return jnp.exp(jnp.sum(jnp.where(inside, total, 0.0), axis=1, keepdims=True))

    own_tail = dot(after, ld, ((1,), (1,)), HIGH)

    def outer(k, weighted):
        hi, lo = halves(weighted)
        return dot(
            jnp.concatenate([k, k], axis=0), jnp.concatenate([hi, lo], axis=0), ((0,), (0,)))

    own = []
    for g in range(kv):
        k_g = k_own[g * tokens:(g + 1) * tokens]
        v_g = v_own[g * tokens:(g + 1) * tokens].astype(F32)
        own.append(outer(k_g, v_g * jnp.exp(own_tail[:, g:g + 1])))

    for o in range(1, n_seq):
        for copy in kv_arrivals(o):
            copy.wait_recv()
    state = [jnp.zeros((width, width), F32) for _ in range(kv)]
    for s in range(n_seq):
        k_s = dot(by_head, kbuf[s]).astype(BF16)
        v_s = dot(by_head, vbuf[s])
        for g in range(kv):
            k_g = k_s[g * tokens:(g + 1) * tokens]
            v_g = v_s[g * tokens:(g + 1) * tokens]
            kd[g, s * tokens:(s + 1) * tokens, :] = k_g
            vd[g, s * tokens:(s + 1) * tokens, :] = v_g.astype(BF16)
            col = s * n_inner * LD_ROWS + g
            state[g] = state[g] + outer(k_g, v_g * far[:, col:col + 1])

    start = z * n_inner
    for g in range(kv):
        msg[0, g] = state[g]
        msg[1, g] = state[g] * span(g, start, me + 1) + own[g]

    def m_copy(o):
        to = lax.rem(x + o, n_inner)
        return pltpu.make_async_remote_copy(
            src_ref=msg.at[jnp.where(to > x, 1, 0)], dst_ref=got.at[o],
            send_sem=m_send.at[o], recv_sem=m_recv.at[o],
            device_id={"inner": to}, device_id_type=MESH)

    for o in range(1, n_inner):
        m_copy(o).start()

    step = min(rows, 256)
    scale = width ** (-0.5) * LOG2E

    @pl.loop(0, rows // step)
    def _(c):
        at = pl.ds(pl.multiple_of(c * step, step), step)
        for g in range(kv):
            score = dot(qs[g, at, :], kd[g], ((1,), (1,))) + bias[at, :]
            top = jnp.max(score, axis=1, keepdims=True)
            expo = jnp.exp2((score - top) * scale)
            denom = jnp.sum(expo, axis=1, keepdims=True)
            sp[g, at, :] = dot(expo.astype(BF16), vd[g]) / denom

    prior = [state[g] * span(g, start, me) for g in range(kv)]
    for o in range(1, n_inner):
        m_copy(o).wait_recv()
        source = lax.rem(x + n_inner - o, n_inner)
        first = jnp.where(source < x, start + source + 1, start)
        for g in range(kv):
            prior[g] = prior[g] + got[o, g] * span(g, first, me)

    done = []
    for g in range(kv):
        hi, lo = halves(prior[g])
        q_g = qs[g]
        inter = dot(
            jnp.concatenate([q_g, q_g], axis=1), jnp.concatenate([hi, lo], axis=0))
        linear = lin[g] + inter * jnp.exp(cum_row[:, g:g + 1])
        norm = lax.rsqrt(jnp.mean(linear * linear, axis=1, keepdims=True) + 1e-6)
        scaled = (linear * norm).reshape(tokens, rep, width) * gain_ref[g * rep:(g + 1) * rep, :][None]
        done.append(scaled + sp[g].reshape(tokens, rep, width))
    out_ref[...] = jnp.concatenate(done, axis=1).astype(out_ref.dtype)

    @pl.loop(1, pieces)
    def _(o):
        ld_copy(o).wait_send()

    for o in range(1, n_seq):
        for copy in kv_copies(o):
            copy.wait_send()
    for o in range(1, n_inner):
        m_copy(o).wait_send()


def shards(n_seq, n_inner, queries, keys, values, log_decay, gain, block_list):
    tokens, heads, width = queries.shape
    kv = keys.shape[1]
    rows = tokens * (heads // kv)
    pieces = n_seq * n_inner
    decay = jnp.pad(log_decay.T, ((0, LD_ROWS - kv), (0, 0)))
    vmem = pl.BlockSpec(memory_space=pltpu.VMEM)
    anywhere = pl.BlockSpec(memory_space=pl.ANY)
    dma = pltpu.SemaphoreType.DMA
    return pl.pallas_call(
        functools.partial(kernel, n_seq, n_inner, kv),
        out_shape=jax.ShapeDtypeStruct(queries.shape, queries.dtype),
        in_specs=[anywhere, anywhere, anywhere, vmem, vmem, vmem],
        out_specs=vmem,
        scratch_shapes=[
            pltpu.VMEM(queries.shape, BF16),
            pltpu.VMEM((n_seq, kv * tokens, width), BF16),
            pltpu.VMEM((n_seq, kv * tokens, width), BF16),
            pltpu.VMEM((pieces, LD_ROWS, tokens), F32),
            pltpu.VMEM((kv, rows, width), BF16),
            pltpu.VMEM((kv, n_seq * tokens, width), BF16),
            pltpu.VMEM((kv, n_seq * tokens, width), BF16),
            pltpu.VMEM((rows, n_seq * tokens), F32),
            pltpu.VMEM((kv, rows, width), F32),
            pltpu.VMEM((kv, rows, width), F32),
            pltpu.VMEM((2, kv, width, width), F32),
            pltpu.VMEM((n_inner, kv, width, width), F32),
            dma((4,)),
            dma((n_seq,)), dma((n_seq,)), dma((n_seq,)), dma((n_seq,)),
            dma((pieces,)), dma((pieces,)),
            dma((n_inner,)), dma((n_inner,)),
        ],
        compiler_params=pltpu.CompilerParams(collective_id=0, has_side_effects=True),
        name="prefill",
    )(
        queries, keys.reshape(tokens * kv, width), values.reshape(tokens * kv, width),
        decay, gain, block_list,
    )


def solution(mesh):
    return jax.shard_map(
        functools.partial(shards, mesh.shape["seq"], mesh.shape["inner"]),
        mesh=mesh,
        in_specs=(
            P(("groups", "seq", "inner"), "head", None),
            P(("groups", "seq", "inner"), "head", None),
            P(("groups", "seq", "inner"), "head", None),
            P(("groups", "seq", "inner"), "head"),
            P("head", None),
            P(("groups", "seq", "inner"), None),
        ),
        out_specs=P(("groups", "seq", "inner"), "head", None),
        check_vma=False,
    )
```

time: 110 us -> 28.4 us (0.26)
  blocking collectives: 52.4 us -> 0 us
  Pallas kernels: 0 us -> 24.7 us
  other arithmetic: 18.3 us -> 0 us
  matrix products: 13.7 us -> 0 us
  between operations: 13.6 us -> 0.01 us
  local copies, waits for them, and re-layouts: 11.2 us -> 3.14 us
    all_gather x3 -> x0, blocking collectives: 52.4 us -> none  [the longest x1 20.6 us: prefix(): everything = jax.tree.map(lambda part: lax.all_gather(part, axis), shard)]
    pallas_call x0 -> x1, Pallas kernels: none -> 24.7 us  [shards(): pl.pallas_call(functools.partial(kernel, n_seq, n_inner, kv), out_shape=j...]
    dot_general x8 -> x0, matrix products: 13.7 us -> none  [the longest x2 4.6 us: one_block(): jnp.einsum('krqju,jukd->qkrd', weights, pv, preferred_element_type=jnp.fl...]
    select_n x9 -> x0, other arithmetic: 8.05 us -> none  [the longest x8 7.94 us: turn(): return jax.tree.map(lambda a, b: jnp.where(reached, a, b), new, before)]
    reduce_sum x2 -> x0, other arithmetic: 4.54 us -> none  [one_block(): denom = jnp.sum(expo, axis=(3, 4))]
    dynamic_slice x4 -> x0, local copies, waits for them, and re-layouts: 2.11 us -> none  [shards(): lax.map(one_block, (q_blocks, picked_keys, picked_values, query_pos, key_...]
    mul x2 -> x0, other arithmetic: 1.73 us -> none  [the longest x1 1.04 us: shards(): kf * tail[:, :, None]]
    gather x2 -> x0, local copies, waits for them, and re-layouts: 1.62 us -> none  [the longest x1 0.87 us: shards(): picked_keys = key_blocks[seg_block]]
  transfers between devices with their start and end apart: 1 -> 0, of which waited for: 0 -> 0; matrix products, arithmetic and copies ran while one was open for 25% -> 0% of each run, Pallas kernels for 0% -> 0%
where the time goes in v1:
time: 28.4 us; the launch traced here: 27.9 us
  Pallas kernels  24.7 us (87%)
  local copies, waits for them, and re-layouts  3.14 us (11%)
    pallas_call x1, Pallas kernels, shards(): pl.pallas_call(functools.partial(kernel, n_seq, n_inner, kv), out_shape=j...  24.7 us
    unnamed x3, local copies, waits for them, and re-layouts  2.55 us
    pad x1, local copies, waits for them, and re-layouts, shards(): decay = jnp.pad(log_decay.T, ((0, LD_ROWS - kv), (0, 0)))  0.6 us

profile of v1, /device:TPU:0, one launch (start us, length us, event | category | flops | bytes accessed | tf_op | source)
XLA Modules:
  0.0 27.9 jit_solution(12388295974396716471)
XLA Ops:
  0.0 0.0 copy-start
  0.0 0.7 %copy-done = f32[128,2]{0,1:T(2,128)S(1)} copy-done((f32[128,2]{0,1:T(2,128)S(1)}, f32[128,2]{0,1:T(2,128)}, u32[]{:S(2)}) %copy-start) | copy-done | bytes 1048
  0.7 0.6 %pad.4.ld_ref = f32[8,128]{1,0:T(8,128)} pad(f32[2,128]{1,0:T(2,128)S(1)} %bitcast.5, f32[]{:T(128)} %constant.2.clone.1), padding=0_6x0_0 | pad | bytes 5124 | tf_op jit(solution)/shard_map/jit(_pad)/pad | solution.py:283
  1.3 24.7 %prefill.1 = bf16[128,16,128]{2,1,0:T(8,128)(2,1)} custom-call(bf16[128,16,128]{2,1,0:T(8,128)(2,1)} %q_hbm.1, bf16[256,128]{1,0:T(8,128)(2,1)} %bitcast.3, bf16[256,128]{1,0:T(8,128)(2,1)} %bitcast.4, f32[8,128]{1,0:T(8,128)} %pad.4.ld_ref, f32[16,128]{1,0:T(8,128)} %gain_ref.1, s32[2,16]{1,0:T(2,128)} %list_ref.1), custom_call_target="tpu_custom_call" | custom-call | tf_op jit(solution)/shard_map/prefill/pallas_call | solution.py:287
  26.0 1.9 %copy.8 = bf16[128,16,128]{2,1,0:T(8,128)(2,1)} copy(bf16[128,16,128]{2,1,0:T(8,128)(2,1)} %prefill.1) | data formatting | bytes 1048576
Async XLA Ops:
  0.0 0.7 %copy-start = (f32[128,2]{0,1:T(2,128)S(1)}, f32[128,2]{0,1:T(2,128)}, u32[]{:S(2)}) copy-start(f32[128,2]{0,1:T(2,128)} %param.9) | copy-start | bytes 3076

commit v2 on v1

v2 whole, which is shorter than its diff:
```python
import functools

import jax
import jax.numpy as jnp
from jax import lax
from jax.experimental import pallas as pl
from jax.experimental.pallas import tpu as pltpu
from jax.sharding import PartitionSpec as P

BLK = 64
HIGH = lax.Precision.HIGHEST
MESH = pl.DeviceIdType.MESH
LD_ROWS = 8
F32 = jnp.float32
BF16 = jnp.bfloat16
LOG2E = 1.4426950408889634


def iota(shape, dim):
    return lax.broadcasted_iota(jnp.int32, shape, dim)


def dot(a, b, dims=((1,), (0,)), precision=None):
    return lax.dot_general(
        a, b, (dims, ((), ())), precision=precision, preferred_element_type=F32
    )


def halves(x):
    hi = x.astype(BF16)
    return hi, (x - hi.astype(F32)).astype(BF16)


def kernel(
    n_seq, n_inner, kv,
    q_hbm, k_hbm, v_hbm, ld_hbm, gain_ref, list_ref,
    out_ref,
    qbuf, kbuf, vbuf, ldbuf, qs, kd, vd, bias, lin, sp, msg, got,
    local_sem, k_send, k_recv, v_send, v_recv, l_send, l_recv, x_send, x_recv,
    m_send, m_recv,
):
    z = lax.axis_index("seq")
    x = lax.axis_index("inner")
    tokens, heads, width = qbuf.shape
    rep = heads // kv
    rows = tokens * rep
    per_piece = tokens // BLK
    keys_all = n_seq * tokens
    has_next, has_last = z < n_seq - 1, z > 0

    ldbuf[...] = jnp.zeros_like(ldbuf)
    q_copy = pltpu.make_async_copy(q_hbm, qbuf, local_sem.at[0])
    k_copy = pltpu.make_async_copy(k_hbm, kbuf.at[0], local_sem.at[1])
    v_copy = pltpu.make_async_copy(v_hbm, vbuf.at[0], local_sem.at[2])
    l_copy = pltpu.make_async_copy(ld_hbm, ldbuf.at[0, 0, 0:kv], local_sem.at[3])
    for copy in (l_copy, k_copy, v_copy, q_copy):
        copy.start()

    barrier = pltpu.get_barrier_semaphore()

    @pl.when(has_next)
    def _():
        pl.semaphore_signal(barrier, inc=1, device_id={"seq": z + 1}, device_id_type=MESH)

    @pl.when(has_last)
    def _():
        pl.semaphore_signal(barrier, inc=1, device_id={"seq": z - 1}, device_id_type=MESH)

    for o in range(1, n_inner):
        pl.semaphore_signal(
            barrier, inc=1, device_id={"inner": lax.rem(x + o, n_inner)}, device_id_type=MESH)
    ends = jnp.where(has_next, 1, 0) + jnp.where(has_last, 1, 0)
    pl.semaphore_wait(barrier, n_inner - 1 + ends)

    def hop(src, dst, send, recv):
        return pltpu.make_async_remote_copy(
            src_ref=src, dst_ref=dst, send_sem=send, recv_sem=recv,
            device_id={"seq": z + 1}, device_id_type=MESH)

    def k_hop(j):
        return hop(
            k_hbm if j == 0 else kbuf.at[j], kbuf.at[j + 1], k_send.at[j], k_recv.at[j + 1])

    def v_hop(j):
        return hop(
            v_hbm if j == 0 else vbuf.at[j], vbuf.at[j + 1], v_send.at[j], v_recv.at[j + 1])

    def l_hop(j):
        return hop(
            ldbuf.at[j, :, 0:kv], ldbuf.at[j + 1, :, 0:kv], l_send.at[j], l_recv.at[j + 1])

    def relay(hops, j):
        @pl.when(z >= j)
        def _():
            hops(j - 1).wait_recv()

        if j < n_seq - 1:

            @pl.when((z >= j) & has_next)
            def _():
                hops(j).start()

    def x_copy(o):
        return pltpu.make_async_remote_copy(
            src_ref=ld_hbm, dst_ref=ldbuf.at[0, n_inner - o, 0:kv], send_sem=x_send.at[o],
            recv_sem=x_recv.at[o], device_id={"inner": lax.rem(x + o, n_inner)},
            device_id_type=MESH)

    @pl.when(has_next)
    def _():
        k_hop(0).start()
        v_hop(0).start()

    for o in range(1, n_inner):
        x_copy(o).start()

    lanes = iota((kv * tokens, kv * tokens), 1)
    subs = iota((kv * tokens, kv * tokens), 0)
    by_head = jnp.where(
        lanes == lax.rem(subs, tokens) * kv + subs // tokens, 1.0, 0.0
    ).astype(BF16)

    l_copy.wait()
    ld = ldbuf[0, 0]
    upto = jnp.where(iota((tokens, tokens), 0) <= iota((tokens, tokens), 1), 1.0, 0.0)
    after = jnp.where(iota((tokens, tokens), 0) < iota((tokens, tokens), 1), 1.0, 0.0)
    cum_lane = dot(ld, upto, precision=HIGH)
    row_tok = iota((rows, tokens), 0) // rep
    lane_tok = iota((rows, tokens), 1)
    seen = row_tok >= lane_tok
    cum_row = dot(jnp.where(seen, 1.0, 0.0), ld, ((1,), (1,)), HIGH)
    own_tail = dot(after, ld, ((1,), (1,)), HIGH)

    def outer(k, weighted):
        hi, lo = halves(weighted)
        return dot(
            jnp.concatenate([k, k], axis=0), jnp.concatenate([hi, lo], axis=0), ((0,), (0,)))

    def split(j):
        k_j = dot(by_head, kbuf[j]).astype(BF16)
        v_j = dot(by_head, vbuf[j])
        out = []
        for g in range(kv):
            k_g = k_j[g * tokens:(g + 1) * tokens]
            v_g = v_j[g * tokens:(g + 1) * tokens]
            kd[g, j * tokens:(j + 1) * tokens, :] = k_g
            vd[g, j * tokens:(j + 1) * tokens, :] = v_g.astype(BF16)
            out.append((k_g, v_g))
        return out

    k_copy.wait()
    v_copy.wait()
    mine = split(0)
    own = [outer(k_g, v_g * jnp.exp(own_tail[:, g:g + 1])) for g, (k_g, v_g) in enumerate(mine)]

    key_lane = iota((1, keys_all), 1)
    key_block = (
        ((z - key_lane // tokens) * n_inner + x) * per_piece + lax.rem(key_lane, tokens) // BLK
    )
    key_pos = key_block * BLK + lax.rem(key_lane, BLK)
    listed = list_ref[...]
    for b in range(per_piece):
        member = key_block == listed[b:b + 1, 0:1]
        for i in range(1, listed.shape[1]):
            member = jnp.logical_or(member, key_block == listed[b:b + 1, i:i + 1])
        limit = jnp.where(member, key_pos, jnp.int32(2**30))
        first = (z * n_inner + x) * tokens + b * BLK
        query = first + iota((BLK * rep, 1), 0) // rep
        bias[b * BLK * rep:(b + 1) * BLK * rep, :] = jnp.where(limit <= query, 0.0, -1e30)

    for o in range(1, n_inner):
        x_copy(o).wait_recv()

    @pl.when(has_next)
    def _():
        l_hop(0).start()

    q_copy.wait()
    qf = qbuf[...].astype(F32)
    for g in range(kv):
        qs[g] = qf[:, g * rep:(g + 1) * rep, :].reshape(rows, width).astype(BF16)

    def within(g):
        k_g, v_g = mine[g][0], mine[g][1].astype(BF16)
        diff = cum_row[:, g:g + 1] - cum_lane[g:g + 1, :]
        weight = jnp.where(seen, jnp.exp(jnp.minimum(diff, 0.0)), 0.0)
        hi, lo = halves(dot(qs[g], k_g, ((1,), (1,))) * weight)
        lin[g] = dot(
            jnp.concatenate([hi, lo], axis=1), jnp.concatenate([v_g, v_g], axis=0))

    state = [jnp.zeros((width, width), F32) for _ in range(kv)]
    gap = [jnp.zeros((1, 1), F32) for _ in range(kv)]

    def totals(j):
        t = jnp.sum(ldbuf[j].reshape(n_inner * LD_ROWS, tokens), axis=1, keepdims=True)
        return [[t[o * LD_ROWS + g:o * LD_ROWS + g + 1, :] for o in range(n_inner)]
                for g in range(kv)]

    for j in range(1, n_seq):

        @pl.when(z < j)
        def _():
            kbuf[j] = jnp.zeros_like(kbuf[j])
            vbuf[j] = jnp.zeros_like(vbuf[j])

        relay(k_hop, j)
        if j == 1:
            within(0)
        relay(v_hop, j)
        relay(l_hop, j)
        if j == 1:
            for g in range(1, kv):
                within(g)
        row = totals(j)
        tail = dot(after, ldbuf[j, 0], ((1,), (1,)), HIGH)
        for g, (k_g, v_g) in enumerate(split(j)):
            rest = gap[g]
            for o in range(1, n_inner):
                rest = rest + jnp.where(x + o < n_inner, row[g][o], 0.0)
            state[g] = state[g] + outer(k_g, v_g * jnp.exp(tail[:, g:g + 1] + rest))
            gap[g] = gap[g] + sum(row[g])

    row = totals(0)
    before = []
    for g in range(kv):
        past = jnp.zeros((1, 1), F32)
        for o in range(1, n_inner):
            past = past + jnp.where(x + o >= n_inner, row[g][o], 0.0)
        before.append(past)
        msg[0, g] = state[g]
        msg[1, g] = state[g] * jnp.exp(past + row[g][0]) + own[g]

    def m_copy(o):
        to = lax.rem(x + o, n_inner)
        return pltpu.make_async_remote_copy(
            src_ref=msg.at[jnp.where(to > x, 1, 0)], dst_ref=got.at[o],
            send_sem=m_send.at[o], recv_sem=m_recv.at[o],
            device_id={"inner": to}, device_id_type=MESH)

    for o in range(1, n_inner):
        m_copy(o).start()

    step = min(rows, 256)
    scale = width ** (-0.5) * LOG2E

    @pl.loop(0, rows // step)
    def _(c):
        at = pl.ds(pl.multiple_of(c * step, step), step)
        for g in range(kv):
            score = dot(qs[g, at, :], kd[g], ((1,), (1,))) + bias[at, :]
            top = jnp.max(score, axis=1, keepdims=True)
            expo = jnp.exp2((score - top) * scale)
            denom = jnp.sum(expo, axis=1, keepdims=True)
            sp[g, at, :] = dot(expo.astype(BF16), vd[g]) / denom

    prior = [state[g] * jnp.exp(before[g]) for g in range(kv)]
    for o in range(1, n_inner):
        m_copy(o).wait_recv()
        for g in range(kv):
            later = jnp.zeros((1, 1), F32)
            for r in range(n_inner - o + 1, n_inner):
                later = later + row[g][r]
            prior[g] = prior[g] + got[o, g] * jnp.exp(jnp.where(x >= o, later, before[g]))

    done = []
    for g in range(kv):
        hi, lo = halves(prior[g])
        q_g = qs[g]
        inter = dot(
            jnp.concatenate([q_g, q_g], axis=1), jnp.concatenate([hi, lo], axis=0))
        linear = lin[g] + inter * jnp.exp(cum_row[:, g:g + 1])
        norm = lax.rsqrt(jnp.mean(linear * linear, axis=1, keepdims=True) + 1e-6)
        scaled = (linear * norm).reshape(tokens, rep, width) * gain_ref[g * rep:(g + 1) * rep, :][None]
        done.append(scaled + sp[g].reshape(tokens, rep, width))
    out_ref[...] = jnp.concatenate(done, axis=1).astype(out_ref.dtype)

    for j in range(n_seq - 1):

        @pl.when((z >= j) & has_next)
        def _():
            for hops in (k_hop, v_hop, l_hop):
                hops(j).wait_send()

    for o in range(1, n_inner):
        x_copy(o).wait_send()
        m_copy(o).wait_send()


def shards(n_seq, n_inner, queries, keys, values, log_decay, gain, block_list):
    tokens, heads, width = queries.shape
    kv = keys.shape[1]
    rows = tokens * (heads // kv)
    vmem = pl.BlockSpec(memory_space=pltpu.VMEM)
    anywhere = pl.BlockSpec(memory_space=pl.ANY)
    dma = pltpu.SemaphoreType.DMA
    return pl.pallas_call(
        functools.partial(kernel, n_seq, n_inner, kv),
        out_shape=jax.ShapeDtypeStruct(queries.shape, queries.dtype),
        in_specs=[anywhere, anywhere, anywhere, anywhere, vmem, vmem],
        out_specs=vmem,
        scratch_shapes=[
            pltpu.VMEM(queries.shape, BF16),
            pltpu.VMEM((n_seq, kv * tokens, width), BF16),
            pltpu.VMEM((n_seq, kv * tokens, width), BF16),
            pltpu.VMEM((n_seq, n_inner, LD_ROWS, tokens), F32),
            pltpu.VMEM((kv, rows, width), BF16),
            pltpu.VMEM((kv, n_seq * tokens, width), BF16),
            pltpu.VMEM((kv, n_seq * tokens, width), BF16),
            pltpu.VMEM((rows, n_seq * tokens), F32),
            pltpu.VMEM((kv, rows, width), F32),
            pltpu.VMEM((kv, rows, width), F32),
            pltpu.VMEM((2, kv, width, width), F32),
            pltpu.VMEM((n_inner, kv, width, width), F32),
            dma((4,)),
            dma((n_seq,)), dma((n_seq,)), dma((n_seq,)), dma((n_seq,)),
            dma((n_seq,)), dma((n_seq,)), dma((n_inner,)), dma((n_inner,)),
            dma((n_inner,)), dma((n_inner,)),
        ],
        compiler_params=pltpu.CompilerParams(collective_id=0, has_side_effects=True),
        name="prefill",
    )(
        queries, keys.reshape(tokens * kv, width), values.reshape(tokens * kv, width),
        log_decay.T, gain, block_list,
    )


def solution(mesh):
    return jax.shard_map(
        functools.partial(shards, mesh.shape["seq"], mesh.shape["inner"]),
        mesh=mesh,
        in_specs=(
            P(("groups", "seq", "inner"), "head", None),
            P(("groups", "seq", "inner"), "head", None),
            P(("groups", "seq", "inner"), "head", None),
            P(("groups", "seq", "inner"), "head"),
            P("head", None),
            P(("groups", "seq", "inner"), None),
        ),
        out_specs=P(("groups", "seq", "inner"), "head", None),
        check_vma=False,
    )
```

time: 28.4 us -> 22.3 us (0.79)
  the two profiles are of different devices: /device:TPU:0 before, /device:TPU:24 now
where the time goes in v2:
time: 22.3 us; the launch traced here: 22.1 us
  Pallas kernels  20.2 us (91%)
  local copies, waits for them, and re-layouts  1.87 us (8%)
    pallas_call x1, Pallas kernels, shards(): pl.pallas_call(functools.partial(kernel, n_seq, n_inner, kv), out_shape=j...  20.2 us
    unnamed x1, local copies, waits for them, and re-layouts  1.87 us

profile of v2, /device:TPU:24, one launch (start us, length us, event | category | flops | bytes accessed | tf_op | source)
XLA Modules:
  0.0 22.1 jit_solution(7297718906558312891)
XLA Ops:
  0.0 20.2 %prefill.1 = bf16[128,16,128]{2,1,0:T(8,128)(2,1)} custom-call(bf16[128,16,128]{2,1,0:T(8,128)(2,1)} %q_hbm.1, bf16[256,128]{1,0:T(8,128)(2,1)} %bitcast.3, bf16[256,128]{1,0:T(8,128)(2,1)} %bitcast.4, f32[2,128]{1,0:T(2,128)} %bitcast.5, f32[16,128]{1,0:T(8,128)} %gain_ref.1, s32[2,16]{1,0:T(2,128)} %list_ref.1), custom_call_target="tpu_custom_call" | custom-call | tf_op jit(solution)/shard_map/prefill/pallas_call | solution.py:296
  20.2 1.9 %copy.8 = bf16[128,16,128]{2,1,0:T(8,128)(2,1)} copy(bf16[128,16,128]{2,1,0:T(8,128)(2,1)} %prefill.1) | data formatting | bytes 1048576

commit v3 on v2

--- a/solution.py
+++ b/solution.py
@@ -35,9 +35,9 @@
     n_seq, n_inner, kv,
     q_hbm, k_hbm, v_hbm, ld_hbm, gain_ref, list_ref,
     out_ref,
-    qbuf, kbuf, vbuf, ldbuf, qs, kd, vd, bias, lin, sp, msg, got,
+    qbuf, kbuf, vbuf, ldbuf, qs, kd, vd, bias, lin, sp, msg, got, own_msg, own_got,
     local_sem, k_send, k_recv, v_send, v_recv, l_send, l_recv, x_send, x_recv,
-    m_send, m_recv,
+    m_send, m_recv, o_send, o_recv,
 ):
     z = lax.axis_index("seq")
     x = lax.axis_index("inner")
@@ -152,21 +152,14 @@
     v_copy.wait()
     mine = split(0)
     own = [outer(k_g, v_g * jnp.exp(own_tail[:, g:g + 1])) for g, (k_g, v_g) in enumerate(mine)]
-
-    key_lane = iota((1, keys_all), 1)
-    key_block = (
-        ((z - key_lane // tokens) * n_inner + x) * per_piece + lax.rem(key_lane, tokens) // BLK
-    )
-    key_pos = key_block * BLK + lax.rem(key_lane, BLK)
-    listed = list_ref[...]
-    for b in range(per_piece):
-        member = key_block == listed[b:b + 1, 0:1]
-        for i in range(1, listed.shape[1]):
-            member = jnp.logical_or(member, key_block == listed[b:b + 1, i:i + 1])
-        limit = jnp.where(member, key_pos, jnp.int32(2**30))
-        first = (z * n_inner + x) * tokens + b * BLK
-        query = first + iota((BLK * rep, 1), 0) // rep
-        bias[b * BLK * rep:(b + 1) * BLK * rep, :] = jnp.where(limit <= query, 0.0, -1e30)
+    for g in range(kv):
+        own_msg[g] = own[g]
+
+    def o_copy(o):
+        return pltpu.make_async_remote_copy(
+            src_ref=own_msg, dst_ref=own_got.at[o], send_sem=o_send.at[o],
+            recv_sem=o_recv.at[o], device_id={"inner": lax.rem(x + o, n_inner)},
+            device_id_type=MESH)
 
     for o in range(1, n_inner):
         x_copy(o).wait_recv()
@@ -175,10 +168,30 @@
     def _():
         l_hop(0).start()
 
-    q_copy.wait()
-    qf = qbuf[...].astype(F32)
-    for g in range(kv):
-        qs[g] = qf[:, g * rep:(g + 1) * rep, :].reshape(rows, width).astype(BF16)
+    for o in range(1, n_inner):
+        o_copy(o).start()
+
+    def visibility():
+        key_lane = iota((1, keys_all), 1)
+        key_block = (
+            ((z - key_lane // tokens) * n_inner + x) * per_piece + lax.rem(key_lane, tokens) // BLK
+        )
+        key_pos = key_block * BLK + lax.rem(key_lane, BLK)
+        listed = list_ref[...]
+        for b in range(per_piece):
+            member = key_block == listed[b:b + 1, 0:1]
+            for i in range(1, listed.shape[1]):
+                member = jnp.logical_or(member, key_block == listed[b:b + 1, i:i + 1])
+            limit = jnp.where(member, key_pos, jnp.int32(2**30))
+            first = (z * n_inner + x) * tokens + b * BLK
+            query = first + iota((BLK * rep, 1), 0) // rep
+            bias[b * BLK * rep:(b + 1) * BLK * rep, :] = jnp.where(limit <= query, 0.0, -1e30)
+
+    def take_queries():
+        q_copy.wait()
+        qf = qbuf[...].astype(F32)
+        for g in range(kv):
+            qs[g] = qf[:, g * rep:(g + 1) * rep, :].reshape(rows, width).astype(BF16)
 
     def within(g):
         k_g, v_g = mine[g][0], mine[g][1].astype(BF16)
@@ -196,21 +209,7 @@
         return [[t[o * LD_ROWS + g:o * LD_ROWS + g + 1, :] for o in range(n_inner)]
                 for g in range(kv)]
 
-    for j in range(1, n_seq):
-
-        @pl.when(z < j)
-        def _():
-            kbuf[j] = jnp.zeros_like(kbuf[j])
-            vbuf[j] = jnp.zeros_like(vbuf[j])
-
-        relay(k_hop, j)
-        if j == 1:
-            within(0)
-        relay(v_hop, j)
-        relay(l_hop, j)
-        if j == 1:
-            for g in range(1, kv):
-                within(g)
+    def absorb(j):
         row = totals(j)
         tail = dot(after, ldbuf[j, 0], ((1,), (1,)), HIGH)
         for g, (k_g, v_g) in enumerate(split(j)):
@@ -220,30 +219,52 @@
             state[g] = state[g] + outer(k_g, v_g * jnp.exp(tail[:, g:g + 1] + rest))
             gap[g] = gap[g] + sum(row[g])
 
+    def first_head():
+        take_queries()
+        within(0)
+
+    work = [visibility, first_head] + [functools.partial(within, g) for g in range(1, kv)]
+    for j in range(1, n_seq):
+
+        @pl.when(z < j)
+        def _():
+            kbuf[j] = jnp.zeros_like(kbuf[j])
+            vbuf[j] = jnp.zeros_like(vbuf[j])
+
+        relay(k_hop, j)
+        if work:
+            work.pop(0)()
+        relay(v_hop, j)
+        relay(l_hop, j)
+        work.append(functools.partial(absorb, j))
+        work.pop(0)()
+    for item in work:
+        item()
+
     row = totals(0)
     before = []
     for g in range(kv):
-        past = jnp.zeros((1, 1), F32)
+        past, ahead = jnp.zeros((1, 1), F32), jnp.zeros((1, 1), F32)
         for o in range(1, n_inner):
             past = past + jnp.where(x + o >= n_inner, row[g][o], 0.0)
+            ahead = ahead + jnp.where(x + o < n_inner, row[g][o], 0.0)
         before.append(past)
-        msg[0, g] = state[g]
-        msg[1, g] = state[g] * jnp.exp(past + row[g][0]) + own[g]
+        msg[g] = state[g] * jnp.exp(sum(row[g])) + own[g] * jnp.exp(ahead)
 
     def m_copy(o):
-        to = lax.rem(x + o, n_inner)
         return pltpu.make_async_remote_copy(
-            src_ref=msg.at[jnp.where(to > x, 1, 0)], dst_ref=got.at[o],
-            send_sem=m_send.at[o], recv_sem=m_recv.at[o],
-            device_id={"inner": to}, device_id_type=MESH)
-
-    for o in range(1, n_inner):
-        m_copy(o).start()
+            src_ref=msg, dst_ref=got.at[o], send_sem=m_send.at[o], recv_sem=m_recv.at[o],
+            device_id={"seq": z + 1, "inner": lax.rem(x + o, n_inner)}, device_id_type=MESH)
+
+    @pl.when(has_next)
+    def _():
+        for o in range(1, n_inner):
+            m_copy(o).start()
 
     step = min(rows, 256)
     scale = width ** (-0.5) * LOG2E
 
-    @pl.loop(0, rows // step)
+    @pl.loop(0, rows // step, unroll=True)
     def _(c):
         at = pl.ds(pl.multiple_of(c * step, step), step)
         for g in range(kv):
@@ -253,14 +274,29 @@
             denom = jnp.sum(expo, axis=1, keepdims=True)
             sp[g, at, :] = dot(expo.astype(BF16), vd[g]) / denom
 
-    prior = [state[g] * jnp.exp(before[g]) for g in range(kv)]
-    for o in range(1, n_inner):
-        m_copy(o).wait_recv()
+
+    @pl.when(has_last)
+    def _():
+        for o in range(1, n_inner):
+            m_copy(o).wait_recv()
+
+    @pl.when(z == 0)
+    def _():
+        got[...] = jnp.zeros_like(got)
+
+    prior = []
+    for g in range(kv):
+        at_row = state[g]
+        for o in range(1, n_inner):
+            at_row = at_row + got[o, g]
+        prior.append(at_row * jnp.exp(before[g]))
+    for o in range(1, n_inner):
+        o_copy(o).wait_recv()
         for g in range(kv):
             later = jnp.zeros((1, 1), F32)
             for r in range(n_inner - o + 1, n_inner):
                 later = later + row[g][r]
-            prior[g] = prior[g] + got[o, g] * jnp.exp(jnp.where(x >= o, later, before[g]))
+            prior[g] = prior[g] + own_got[o, g] * jnp.where(x >= o, jnp.exp(later), 0.0)
 
     done = []
     for g in range(kv):
@@ -283,7 +319,12 @@
 
     for o in range(1, n_inner):
         x_copy(o).wait_send()
-        m_copy(o).wait_send()
+        o_copy(o).wait_send()
+
+    @pl.when(has_next)
+    def _():
+        for o in range(1, n_inner):
+            m_copy(o).wait_send()
 
 
 def shards(n_seq, n_inner, queries, keys, values, log_decay, gain, block_list):
@@ -309,12 +350,14 @@
             pltpu.VMEM((rows, n_seq * tokens), F32),
             pltpu.VMEM((kv, rows, width), F32),
             pltpu.VMEM((kv, rows, width), F32),
-            pltpu.VMEM((2, kv, width, width), F32),
+            pltpu.VMEM((kv, width, width), F32),
+            pltpu.VMEM((n_inner, kv, width, width), F32),
+            pltpu.VMEM((kv, width, width), F32),
             pltpu.VMEM((n_inner, kv, width, width), F32),
             dma((4,)),
             dma((n_seq,)), dma((n_seq,)), dma((n_seq,)), dma((n_seq,)),
             dma((n_seq,)), dma((n_seq,)), dma((n_inner,)), dma((n_inner,)),
-            dma((n_inner,)), dma((n_inner,)),
+            dma((n_inner,)), dma((n_inner,)), dma((n_inner,)), dma((n_inner,)),
         ],
         compiler_params=pltpu.CompilerParams(collective_id=0, has_side_effects=True),
         name="prefill",

time: 22.3 us -> 21.9 us (0.982)
  the two profiles are of different devices: /device:TPU:24 before, /device:TPU:30 now
where the time goes in v3:
time: 21.9 us; the launch traced here: 21.6 us
  Pallas kernels  19.8 us (90%)
  local copies, waits for them, and re-layouts  1.87 us (9%)
    pallas_call x1, Pallas kernels, shards(): pl.pallas_call(functools.partial(kernel, n_seq, n_inner, kv), out_shape=j...  19.8 us
    unnamed x1, local copies, waits for them, and re-layouts  1.87 us

profile of v3, /device:TPU:30, one launch (start us, length us, event | category | flops | bytes accessed | tf_op | source)
XLA Modules:
  0.0 21.6 jit_solution(5440382339071990978)
XLA Ops:
  0.0 19.8 %prefill.1 = bf16[128,16,128]{2,1,0:T(8,128)(2,1)} custom-call(bf16[128,16,128]{2,1,0:T(8,128)(2,1)} %q_hbm.1, bf16[256,128]{1,0:T(8,128)(2,1)} %bitcast.3, bf16[256,128]{1,0:T(8,128)(2,1)} %bitcast.4, f32[2,128]{1,0:T(2,128)} %bitcast.5, f32[16,128]{1,0:T(8,128)} %gain_ref.1, s32[2,16]{1,0:T(2,128)} %list_ref.1), custom_call_target="tpu_custom_call" | custom-call | tf_op jit(solution)/shard_map/prefill/pallas_call | solution.py:337
  19.8 1.9 %copy.8 = bf16[128,16,128]{2,1,0:T(8,128)(2,1)} copy(bf16[128,16,128]{2,1,0:T(8,128)(2,1)} %prefill.1) | data formatting | bytes 1048576

commit v4 on v3

--- a/solution.py
+++ b/solution.py
@@ -261,7 +261,7 @@
         for o in range(1, n_inner):
             m_copy(o).start()
 
-    step = min(rows, 256)
+    step = min(rows, 512)
     scale = width ** (-0.5) * LOG2E
 
     @pl.loop(0, rows // step, unroll=True)

time: 21.9 us -> 21.1 us (0.963)
  the two profiles are of different devices: /device:TPU:30 before, /device:TPU:28 now
where the time goes in v4:
time: 21.1 us; the launch traced here: 20.9 us
  Pallas kernels  19 us (90%)
  local copies, waits for them, and re-layouts  1.87 us (9%)
    pallas_call x1, Pallas kernels, shards(): pl.pallas_call(functools.partial(kernel, n_seq, n_inner, kv), out_shape=j...  19 us
    unnamed x1, local copies, waits for them, and re-layouts  1.87 us

profile of v4, /device:TPU:28, one launch (start us, length us, event | category | flops | bytes accessed | tf_op | source)
XLA Modules:
  0.0 20.9 jit_solution(10786717348841831084)
XLA Ops:
  0.0 19.0 %prefill.1 = bf16[128,16,128]{2,1,0:T(8,128)(2,1)} custom-call(bf16[128,16,128]{2,1,0:T(8,128)(2,1)} %q_hbm.1, bf16[256,128]{1,0:T(8,128)(2,1)} %bitcast.3, bf16[256,128]{1,0:T(8,128)(2,1)} %bitcast.4, f32[2,128]{1,0:T(2,128)} %bitcast.5, f32[16,128]{1,0:T(8,128)} %gain_ref.1, s32[2,16]{1,0:T(2,128)} %list_ref.1), custom_call_target="tpu_custom_call" | custom-call | tf_op jit(solution)/shard_map/prefill/pallas_call | solution.py:337
  19.0 1.9 %copy.8 = bf16[128,16,128]{2,1,0:T(8,128)(2,1)} copy(bf16[128,16,128]{2,1,0:T(8,128)(2,1)} %prefill.1) | data formatting | bytes 1048576
